TPU v7x, 256 devices: a whole 4x4x8 slice. The times are simulated.
256 devices in a mesh: row: 32 (over z, y), col: 8 (over x, core).
Axes of the slice: x: 4, y: 4, z: 8, core: 2. Of those that a mesh axis runs over, the one named last changes fastest.
Arguments:
- inputs: bfloat16 [1024, 12288], P('row', 'col'), may hold values from -6 to 6
- hidden_pre: bfloat16 [1024, 24576], P(None, 'row'), may hold values from -8 to 8
- out_grad: bfloat16 [1024, 12288], P('row', 'col'), may hold values from -6 to 6
- weight_in: bfloat16 [12288, 24576], P('col', 'row'), may hold values from -0.0546875 to 0.0546875
- weight_out: bfloat16 [24576, 12288], P('row', 'col'), may hold values from -0.0390625 to 0.0390625
Outputs:
- grad_in: bfloat16 [1024, 12288], P('row', 'col')
- grad_weight_in: bfloat16 [12288, 24576], P('col', 'row')
- grad_weight_out: bfloat16 [24576, 12288], P('row', 'col')
All inputs are finite; a program needn't handle non-finite values.
Results may differ from a plain program's by a relative error of at most 0.0049.
Values may be sent and summed in bfloat16 or wider, within the bound.
A program may use at most 128 MiB of HBM per device.

v0:
```python
import jax
import jax.numpy as jnp
from jax import lax
from jax.sharding import PartitionSpec as P


def gelu_parts(hidden_pre):
    hval = hidden_pre.astype(jnp.float32)
    inner = 0.7978845608 * (hval + 0.044715 * hval * hval * hval)
    tval = jnp.tanh(inner)
    act = 0.5 * hval * (1.0 + tval)
    slope = 0.5 * (1.0 + tval) + 0.5 * hval * (1.0 - tval * tval) * 0.7978845608 * (
        1.0 + 3.0 * 0.044715 * hval * hval
    )
    return (act, slope)


def contract_rows(left, right):
    return lax.dot_general(
        left, right, (((0,), (0,)), ((), ())), preferred_element_type=jnp.float32
    )


def contract_cols(left, right):
    return lax.dot_general(
        left, right, (((1,), (1,)), ((), ())), preferred_element_type=jnp.float32
    )


def body(inputs, hidden_pre, out_grad, weight_in, weight_out):
    act, slope = gelu_parts(hidden_pre)
    act_b = act.astype(jnp.bfloat16)
    grad_all, input_all = (
        lax.all_gather(out_grad, "row", axis=0, tiled=True),
        lax.all_gather(inputs, "row", axis=0, tiled=True),
    )
    grad_weight_out = contract_rows(act_b, grad_all).astype(jnp.bfloat16)
    col_rows = grad_all.shape[0] // lax.axis_size("col")
    piece = grad_all
    d_act = lax.psum_scatter(
        contract_cols(piece, weight_out), "col", scatter_dimension=0, tiled=True
    )
    slope_mine = lax.dynamic_slice_in_dim(slope, lax.axis_index("col") * col_rows, col_rows, 0)
    d_mine = (d_act * slope_mine).astype(jnp.bfloat16)
    d_hid = lax.all_gather(d_mine, "col", axis=0, tiled=True)
    piece = d_hid
    grad_in = lax.psum_scatter(
        contract_cols(piece, weight_in), "row", scatter_dimension=0, tiled=True
    ).astype(jnp.bfloat16)
    grad_weight_in = contract_rows(input_all, d_hid).astype(jnp.bfloat16)
    return (grad_in, grad_weight_in, grad_weight_out)


def solution(mesh):
    return jax.shard_map(
        body,
        mesh=mesh,
        in_specs=(
            P("row", "col"),
            P(None, "row"),
            P("row", "col"),
            P("col", "row"),
            P("row", "col"),
        ),
        out_specs=(P("row", "col"), P("col", "row"), P("row", "col")),
        check_vma=False,
    )
```

profile of v0, /device:TPU:2, one launch (start us, length us, event | category | flops | bytes accessed | tf_op | source)
XLA Modules:
  0.0 481.1 jit_solution(16308524493274345741)
XLA Ops:
  7.2 0.0 copy-start
  7.2 0.0 all-gather.4.cloned.1.call-start
  7.2 0.7 all-gather.4.cloned.1.call-update
  7.9 0.0 reduce-scatter.3.cloned.1.call-start
  8.0 85.1 %all-gather.4.cloned.1.call-done = bf16[1024,1536]{1,0:T(8,128)(2,1)} async-done(((bf16[32,1536]{1,0:T(8,128)(2,1)}), bf16[1024,1536]{1,0:T(8,128)(2,1)}) %all-gather.4.cloned.1.call-update) | async-done | bytes 3145744 | tf_op jit(solution)/shard_map/all_gather | solution.py:34
  93.0 6.9 %fusion.12 = f32[1024,768]{1,0:T(8,128)} fusion(bf16[1024,1536]{1,0:T(8,128)(2,1)} %all-gather.4.cloned.1.call-done, bf16[768,1536]{1,0:T(8,128)(2,1)} %param.9), kind=kOutput, calls=%fused_computation.21 | convolution fusion | flops 2415919104 | bytes 8650752 | tf_op jit(solution)/shard_map/dot_general | solution.py:25
  99.9 0.0 reduce-scatter.3.cloned.1.call-update
  99.9 0.0 all-gather.6.cloned.1.call-start
  100.0 3.3 convert_element_type.21
  103.3 6.0 %fusion.1 = (f32[1024,768]{1,0:T(8,128)}, f32[1024,768]{1,0:T(8,128)}, f32[1024,768]{1,0:T(8,128)}) fusion(bf16[1024,768]{1,0:T(8,128)(2,1)} %param.6), kind=kLoop, calls=%fused_computation.4 | loop fusion | flops 6291456 | bytes 11010048 | tf_op jit(solution)/shard_map/tanh | solution.py:10
  109.2 22.6 %reduce-scatter.3.cloned.1.call-done = f32[128,768]{1,0:T(8,128)} async-done(((f32[1024,768]{1,0:T(8,128)}), f32[128,768]{1,0:T(8,128)}) %reduce-scatter.3.cloned.1.call-update) | async-done | bytes 393232 | tf_op jit(solution)/shard_map/reduce_scatter | solution.py:40
  131.9 2.3 fusion.7
  134.2 0.0 all-gather.6.cloned.1.call-update
  134.2 0.0 all-gather.8.cloned.1.call-start
  134.3 0.5 all-gather.8.cloned.1.call-update
  134.8 0.0 reduce-scatter.5.cloned.1.call-start
  134.8 27.0 %all-gather.6.cloned.1.call-done = bf16[1024,768]{1,0:T(8,128)(2,1)} async-done(((bf16[128,768]{1,0:T(8,128)(2,1)}), bf16[1024,768]{1,0:T(8,128)(2,1)}) %all-gather.6.cloned.1.call-update) | async-done | bytes 1572880 | tf_op jit(solution)/shard_map/all_gather | solution.py:45
  161.8 0.0 copy-done
  161.8 6.0 %fusion.13 = f32[1024,1536]{1,0:T(8,128)} fusion(bf16[1024,768]{1,0:T(8,128)(2,1)} %all-gather.6.cloned.1.call-done, bf16[1536,768]{1,0:T(8,128)(2,1)S(1)} %copy-done), kind=kOutput, calls=%fused_computation.22 | convolution fusion | flops 2415919104 | bytes 10223616 | tf_op jit(solution)/shard_map/dot_general | solution.py:25
  167.8 0.0 reduce-scatter.5.cloned.1.call-update
  167.8 6.7 %convolution_convert_fusion = bf16[768,1536]{1,0:T(8,128)(2,1)} fusion(bf16[1024,1536]{1,0:T(8,128)(2,1)} %all-gather.4.cloned.1.call-done, bf16[1024,768]{1,0:T(8,128)(2,1)} %param.6), kind=kOutput, calls=%fused_computation.1 | convolution fusion | flops 2424963072 | bytes 7077888 | tf_op jit(solution)/shard_map/dot_general | solution.py:19
  174.5 71.0 %all-gather.8.cloned.1.call-done = bf16[1024,1536]{1,0:T(8,128)(2,1)} async-done(((bf16[32,1536]{1,0:T(8,128)(2,1)}), bf16[1024,1536]{1,0:T(8,128)(2,1)}) %all-gather.8.cloned.1.call-update) | async-done | bytes 3145744 | tf_op jit(solution)/shard_map/all_gather | solution.py:35
  245.5 6.5 %fusion.2 = bf16[1536,768]{0,1:T(8,128)(2,1)} fusion(bf16[1024,768]{1,0:T(8,128)(2,1)} %all-gather.6.cloned.1.call-done, bf16[1024,1536]{1,0:T(8,128)(2,1)} %all-gather.8.cloned.1.call-done), kind=kOutput, calls=%fused_computation.6 | convolution fusion | flops 2417098752 | bytes 7077888 | tf_op jit(solution)/shard_map/dot_general | solution.py:19
  252.0 4.3 copy.8
  256.3 216.7 %reduce-scatter.5.cloned.1.call-done = f32[32,1536]{1,0:T(8,128)} async-done(((f32[1024,1536]{1,0:T(8,128)}), f32[32,1536]{1,0:T(8,128)}) %reduce-scatter.5.cloned.1.call-update) | async-done | bytes 196624 | tf_op jit(solution)/shard_map/reduce_scatter | solution.py:47
  473.0 1.6 convert_element_type.23
Async XLA Ops:
  7.2 154.6 %copy-start = (bf16[1536,768]{1,0:T(8,128)(2,1)S(1)}, bf16[1536,768]{1,0:T(8,128)(2,1)}, u32[]{:S(2)}) copy-start(bf16[1536,768]{1,0:T(8,128)(2,1)} %param.8) | copy-start | bytes 7077892
  7.2 85.8 %all-gather.4.cloned.1.call-start = ((), (), s32[]{:S(2)}) async-start(), calls=%async_computation.2 | async-start | bytes 3244032 | tf_op jit(solution)/shard_map/all_gather | solution.py:34
  7.9 124.0 %reduce-scatter.3.cloned.1.call-start = ((), (), s32[]{:S(2)}) async-start(), calls=%async_computation.3 | async-start | bytes 3538944 | tf_op jit(solution)/shard_map/reduce_scatter | solution.py:40
  99.9 61.9 %all-gather.6.cloned.1.call-start = ((), (), s32[]{:S(2)}) async-start(), calls=%async_computation.4 | async-start | bytes 1769472 | tf_op jit(solution)/shard_map/all_gather | solution.py:45
  134.2 111.3 %all-gather.8.cloned.1.call-start = ((), (), s32[]{:S(2)}) async-start(), calls=%async_computation.6 | async-start | bytes 3244032 | tf_op jit(solution)/shard_map/all_gather | solution.py:35
  134.8 338.2 %reduce-scatter.5.cloned.1.call-start = ((), (), s32[]{:S(2)}) async-start(), calls=%async_computation.5 | async-start | bytes 6488064 | tf_op jit(solution)/shard_map/reduce_scatter | solution.py:47
Sparse Core Ops, SparseCore 0:
  10.6 82.4 all-gather.3
  100.0 31.7 reduce-scatter.2
  134.3 27.4 all-gather.5
  164.2 81.2 all-gather.7
  249.3 223.5 reduce-scatter.4
where the time goes:
time: 481 us
  waiting for transfers between devices  424 us (88%)
  matrix products  26.1 us (5%)
  between operations  13.8 us (3%)
  other arithmetic  13.1 us (3%)
    reduce_scatter x1, waiting for transfers between devices, body(): lax.psum_scatter(contract_cols(piece, weight_in), 'row', scatter_dimensio...  217 us
    all_gather x1, waiting for transfers between devices, body(): lax.all_gather(out_grad, 'row', axis=0, tiled=True)  85.1 us
    all_gather x1, waiting for transfers between devices, body(): lax.all_gather(inputs, 'row', axis=0, tiled=True)  71 us
    all_gather x1, waiting for transfers between devices, body(): d_hid = lax.all_gather(d_mine, 'col', axis=0, tiled=True)  27 us
    reduce_scatter x1, waiting for transfers between devices, body(): lax.psum_scatter(contract_cols(piece, weight_out), 'col', scatter_dimensi...  22.6 us
    dot_general x2, matrix products, contract_rows(): lax.dot_general(left, right, (((0,), (0,)), ((), ())), preferred_element_...  13.2 us
    dot_general x2, matrix products, contract_cols(): lax.dot_general(left, right, (((1,), (1,)), ((), ())), preferred_element_...  12.9 us
  transfers between devices with their start and end apart: 5, of which 5 were waited for; matrix products, arithmetic and copies ran while one was open for 7% of the time, Pallas kernels for 0%

commit v1 on v0

--- a/solution.py
+++ b/solution.py
@@ -32,7 +32,9 @@
     act_b = act.astype(jnp.bfloat16)
     grad_all, input_all = (
         lax.all_gather(out_grad, "row", axis=0, tiled=True),
-        lax.all_gather(inputs, "row", axis=0, tiled=True),
+        jnp.concatenate(
+            lax.all_to_all(jnp.stack([inputs] * lax.axis_size("row")), "row", 0, 0), axis=0
+        ),
     )
     grad_weight_out = contract_rows(act_b, grad_all).astype(jnp.bfloat16)
     col_rows = grad_all.shape[0] // lax.axis_size("col")

time: 481 us -> 434 us (0.902)
  waiting for transfers between devices: 424 us -> 364 us
  starting transfers between devices: 0.2 us -> 10.1 us
    all_to_all x0 -> x1, waiting for transfers between devices: none -> 83.1 us  [body(): lax.all_to_all(jnp.stack([inputs] * lax.axis_size('row')), 'row', 0, 0)]
    reduce_scatter x1, waiting for transfers between devices: 217 us -> 144 us  [body(): lax.psum_scatter(contract_cols(piece, weight_in), 'row', scatter_dimensio...]
    all_gather x1 -> x0, waiting for transfers between devices: 71 us -> none  [body(): lax.all_gather(inputs, 'row', axis=0, tiled=True)]
    all_to_all x0 -> x1, starting transfers between devices: none -> 9.97 us  [body(): lax.all_to_all(jnp.stack([inputs] * lax.axis_size('row')), 'row', 0, 0)]
where the time goes in v1:
time: 434 us
  waiting for transfers between devices  364 us (84%)
  matrix products  26.2 us (6%)
  between operations  13.8 us (3%)
  other arithmetic  13.1 us (3%)
  starting transfers between devices  10.1 us (2%)
  local copies, waits for them, and re-layouts  7.13 us (2%)
    reduce_scatter x1, waiting for transfers between devices, body(): lax.psum_scatter(contract_cols(piece, weight_in), 'row', scatter_dimensio...  144 us
    all_gather x1, waiting for transfers between devices, body(): lax.all_gather(out_grad, 'row', axis=0, tiled=True)  85.1 us
    all_to_all x1, waiting for transfers between devices, body(): lax.all_to_all(jnp.stack([inputs] * lax.axis_size('row')), 'row', 0, 0)  83.1 us
    all_gather x1, waiting for transfers between devices, body(): d_hid = lax.all_gather(d_mine, 'col', axis=0, tiled=True)  27.6 us
    reduce_scatter x1, waiting for transfers between devices, body(): lax.psum_scatter(contract_cols(piece, weight_out), 'col', scatter_dimensi...  22.6 us
    dot_general x2, matrix products, contract_rows(): lax.dot_general(left, right, (((0,), (0,)), ((), ())), preferred_element_...  13.4 us
    dot_general x2, matrix products, contract_cols(): lax.dot_general(left, right, (((1,), (1,)), ((), ())), preferred_element_...  12.9 us
    all_to_all x1, starting transfers between devices, body(): lax.all_to_all(jnp.stack([inputs] * lax.axis_size('row')), 'row', 0, 0)  9.97 us
  transfers between devices with their start and end apart: 5, of which 5 were waited for; matrix products, arithmetic and copies ran while one was open for 7% of the time, Pallas kernels for 0%

profile of v1, /device:TPU:2, one launch (start us, length us, event | category | flops | bytes accessed | tf_op | source)
XLA Modules:
  0.0 434.0 jit_solution(12248637358237895837)
XLA Ops:
  7.2 0.0 copy-start
  7.2 0.0 all-gather.3.cloned.1.call-start
  7.2 0.7 all-gather.3.cloned.1.call-update
  7.9 0.0 reduce-scatter.3.cloned.1.call-start
  8.0 85.1 %all-gather.3.cloned.1.call-done = bf16[1024,1536]{1,0:T(8,128)(2,1)} async-done(((bf16[32,1536]{1,0:T(8,128)(2,1)}), bf16[1024,1536]{1,0:T(8,128)(2,1)}) %all-gather.3.cloned.1.call-update) | async-done | bytes 3145744 | tf_op jit(solution)/shard_map/all_gather | solution.py:34
  93.0 6.9 %fusion.12 = f32[1024,768]{1,0:T(8,128)} fusion(bf16[1024,1536]{1,0:T(8,128)(2,1)} %all-gather.3.cloned.1.call-done, bf16[768,1536]{1,0:T(8,128)(2,1)} %param.9), kind=kOutput, calls=%fused_computation.21 | convolution fusion | flops 2415919104 | bytes 8650752 | tf_op jit(solution)/shard_map/dot_general | solution.py:25
  99.9 0.0 reduce-scatter.3.cloned.1.call-update
  99.9 0.0 all-gather.5.cloned.1.call-start
  100.0 3.3 convert_element_type.21
  103.3 6.0 %fusion.1 = (f32[1024,768]{1,0:T(8,128)}, f32[1024,768]{1,0:T(8,128)}, f32[1024,768]{1,0:T(8,128)}) fusion(bf16[1024,768]{1,0:T(8,128)(2,1)} %param.6), kind=kLoop, calls=%fused_computation.4 | loop fusion | flops 6291456 | bytes 11010048 | tf_op jit(solution)/shard_map/tanh | solution.py:10
  109.2 22.6 %reduce-scatter.3.cloned.1.call-done = f32[128,768]{1,0:T(8,128)} async-done(((f32[1024,768]{1,0:T(8,128)}), f32[128,768]{1,0:T(8,128)}) %reduce-scatter.3.cloned.1.call-update) | async-done | bytes 393232 | tf_op jit(solution)/shard_map/reduce_scatter | solution.py:42
  131.9 2.3 fusion.7
  134.2 0.0 all-gather.5.cloned.1.call-update
  134.2 0.0 reduce-scatter.5.cloned.1.call-start
  134.3 27.6 %all-gather.5.cloned.1.call-done = bf16[1024,768]{1,0:T(8,128)(2,1)} async-done(((bf16[128,768]{1,0:T(8,128)(2,1)}), bf16[1024,768]{1,0:T(8,128)(2,1)}) %all-gather.5.cloned.1.call-update) | async-done | bytes 1572880 | tf_op jit(solution)/shard_map/all_gather | solution.py:47
  161.8 0.0 copy-done
  161.8 6.0 %fusion.13 = f32[1024,1536]{1,0:T(8,128)} fusion(bf16[1024,768]{1,0:T(8,128)(2,1)} %all-gather.5.cloned.1.call-done, bf16[1536,768]{1,0:T(8,128)(2,1)S(1)} %copy-done), kind=kOutput, calls=%fused_computation.22 | convolution fusion | flops 2415919104 | bytes 10223616 | tf_op jit(solution)/shard_map/dot_general | solution.py:25
  167.8 0.0 copy-start.1
  167.8 0.0 reduce-scatter.5.cloned.1.call-update
  167.8 0.9 copy-done.1
  168.7 2.0 stack.2
  170.7 10.0 %all-to-all-start = ((bf16[32,32,1536]{2,1,0:T(8,128)(2,1)}), bf16[32,32,1536]{2,1,0:T(8,128)(2,1)}, u32[]{:S(2)}, u32[]{:S(2)}) async-start(bf16[32,32,1536]{2,1,0:T(8,128)(2,1)} %stack.2), calls=%async_computation.2 | async-start | bytes 6291456 | tf_op jit(solution)/shard_map/all_to_all | solution.py:36
  180.6 6.9 %convolution_convert_fusion = bf16[768,1536]{1,0:T(8,128)(2,1)} fusion(bf16[1024,1536]{1,0:T(8,128)(2,1)} %all-gather.3.cloned.1.call-done, bf16[1024,768]{1,0:T(8,128)(2,1)} %param.6), kind=kOutput, calls=%fused_computation.1 | convolution fusion | flops 2424963072 | bytes 7077888 | tf_op jit(solution)/shard_map/dot_general | solution.py:19
  187.5 83.1 %all-to-all-done = bf16[32,32,1536]{2,1,0:T(8,128)(2,1)} async-done(((bf16[32,32,1536]{2,1,0:T(8,128)(2,1)}), bf16[32,32,1536]{2,1,0:T(8,128)(2,1)}, u32[]{:S(2)}, u32[]{:S(2)}) %all-to-all-start) | async-done | bytes 3145760 | tf_op jit(solution)/shard_map/all_to_all | solution.py:36
  270.6 6.5 %fusion.2 = bf16[1536,768]{0,1:T(8,128)(2,1)} fusion(bf16[1024,768]{1,0:T(8,128)(2,1)} %all-gather.5.cloned.1.call-done, bf16[1024,1536]{1,0:T(8,128)(2,1)} %bitcast), kind=kOutput, calls=%fused_computation.6 | convolution fusion | flops 2417098752 | bytes 7077888 | tf_op jit(solution)/shard_map/dot_general | solution.py:19
  277.1 4.3 copy.8
  281.4 144.5 %reduce-scatter.5.cloned.1.call-done = f32[32,1536]{1,0:T(8,128)} async-done(((f32[1024,1536]{1,0:T(8,128)}), f32[32,1536]{1,0:T(8,128)}) %reduce-scatter.5.cloned.1.call-update) | async-done | bytes 196624 | tf_op jit(solution)/shard_map/reduce_scatter | solution.py:49
  425.9 1.6 convert_element_type.23
Async XLA Ops:
  7.2 154.6 %copy-start = (bf16[1536,768]{1,0:T(8,128)(2,1)S(1)}, bf16[1536,768]{1,0:T(8,128)(2,1)}, u32[]{:S(2)}) copy-start(bf16[1536,768]{1,0:T(8,128)(2,1)} %param.8) | copy-start | bytes 7077892
  7.2 85.8 %all-gather.3.cloned.1.call-start = ((), (), s32[]{:S(2)}) async-start(), calls=%async_computation.3 | async-start | bytes 3244032 | tf_op jit(solution)/shard_map/all_gather | solution.py:34
  7.9 124.0 %reduce-scatter.3.cloned.1.call-start = ((), (), s32[]{:S(2)}) async-start(), calls=%async_computation.4 | async-start | bytes 3538944 | tf_op jit(solution)/shard_map/reduce_scatter | solution.py:42
  99.9 61.9 %all-gather.5.cloned.1.call-start = ((), (), s32[]{:S(2)}) async-start(), calls=%async_computation.5 | async-start | bytes 1769472 | tf_op jit(solution)/shard_map/all_gather | solution.py:47
  134.2 291.7 %reduce-scatter.5.cloned.1.call-start = ((), (), s32[]{:S(2)}) async-start(), calls=%async_computation.6 | async-start | bytes 6488064 | tf_op jit(solution)/shard_map/reduce_scatter | solution.py:49
  167.8 0.9 copy-start.1
  170.7 100.0 %all-to-all-start = ((bf16[32,32,1536]{2,1,0:T(8,128)(2,1)}), bf16[32,32,1536]{2,1,0:T(8,128)(2,1)}, u32[]{:S(2)}, u32[]{:S(2)}) async-start(bf16[32,32,1536]{2,1,0:T(8,128)(2,1)} %stack.2), calls=%async_computation.2 | async-start | bytes 6291456 | tf_op jit(solution)/shard_map/all_to_all | solution.py:36
Sparse Core Ops, SparseCore 0:
  10.6 82.4 all-gather.2
  100.0 31.7 reduce-scatter.2
  134.3 27.4 all-gather.4
  167.9 257.8 reduce-scatter.4
